TPU v7x, 128 devices: a whole 4x4x4 slice. The times are simulated.
128 devices in a mesh: seq: 16 (over x, y), cand: 8 (over z, core).
Axes of the slice: x: 4, y: 4, z: 4, core: 2. Of those that a mesh axis runs over, the one named last changes fastest.
Arguments:
- behaviors: float32 [8, 131072, 128], P('cand', 'seq'), may hold values from -15 to 15
- cluster_ids: int32 [8, 131072], P('cand', 'seq'), may hold values from 0 to 2047, as said below
- lengths: int32 [8, 16], P('cand', 'seq'), may hold values from 2048 to 8192
- candidates: bfloat16 [8, 4096, 128], P(None, ('seq', 'cand')), may hold values from -6 to 6
- w_query: bfloat16 [128, 128], replicated, may hold values from -0.5 to 0.5
- w_key: bfloat16 [128, 128], replicated, may hold values from -0.5 to 0.5
- w_hidden: bfloat16 [256, 512], replicated, may hold values from -0.375 to 0.375
- b_hidden: float32 [512], replicated, may hold values from -0.5 to 0.5
- w_out: float32 [512], replicated, may hold values from -0.25 to 0.25
Outputs:
- ranking: float32 [8, 4096], P(None, ('seq', 'cand'))
Inputs may be any that keep to these rules, and one draw needn't show every extreme that they name: `cluster_ids`: each user's first 2048 slots name 2048 different clusters.
All inputs are finite; a program needn't handle non-finite values.
Results may differ from a plain program's by a relative error of at most 0.02.
Values may be sent and summed in bfloat16 or wider, within the bound.
A program may use at most 64 MiB of HBM per device.

v0:
```python
import jax
import jax.numpy as jnp
from jax import lax
from jax.sharding import PartitionSpec as P

C = 2048


def cluster_partials(item_rows, cluster_ids, length):
    slots = item_rows.shape[0]
    block_rows = min(512, slots)
    labels = jnp.arange(C, dtype=jnp.int32)

    def accumulate(carry, number):
        totals, tallies = carry
        offset = number * block_rows
        piece = lax.dynamic_slice_in_dim(item_rows, offset, block_rows, 0)
        idents = lax.dynamic_slice_in_dim(cluster_ids, offset, block_rows, 0)
        inside = offset + jnp.arange(block_rows, dtype=jnp.int32) < length
        onehot = ((idents[:, None] == labels[None, :]) & inside[:, None]).astype(jnp.bfloat16)
        upper = lax.optimization_barrier(piece.astype(jnp.bfloat16))
        lower = (piece - upper.astype(jnp.float32)).astype(jnp.bfloat16)
        dims = (((0,), (0,)), ((), ()))
        totals = totals + lax.dot_general(onehot, upper, dims, preferred_element_type=jnp.float32)
        totals = totals + lax.dot_general(onehot, lower, dims, preferred_element_type=jnp.float32)
        tallies = tallies + jnp.sum(onehot, axis=0, dtype=jnp.float32)
        return ((totals, tallies), None)

    start = (jnp.zeros((C, item_rows.shape[1]), jnp.float32), jnp.zeros((C,), jnp.float32))
    (totals, tallies), _ = lax.scan(
        accumulate, start, jnp.arange(slots // block_rows, dtype=jnp.int32)
    )
    return (totals, tallies)


def statistics(sums, counts):
    centroids = (sums / jnp.maximum(counts, 1.0)[..., None]).astype(jnp.bfloat16)
    size_bias = jnp.where(counts > 0, jnp.log(1.0 + counts), jnp.float32(-1000000000.0)).astype(
        jnp.bfloat16
    )
    return (centroids, size_bias)


def make_keys(centroids, w_key):
    return jnp.einsum("ukd,de->uke", centroids, w_key, preferred_element_type=jnp.float32).astype(
        jnp.bfloat16
    )


def rank_rows(candidates, key_rows, centroids, size_bias, w_query, w_hidden, b_hidden, w_out):
    users, local_cands, width = candidates.shape
    queries = jnp.dot(
        candidates.reshape(users * local_cands, width), w_query, preferred_element_type=jnp.float32
    )
    queries = queries.astype(jnp.bfloat16).reshape(users, local_cands, width)
    scores = jnp.einsum(
        "ucd,ukd->uck", queries, key_rows, preferred_element_type=jnp.float32
    ) / jnp.sqrt(jnp.float32(width))
    scores = scores + size_bias.astype(jnp.float32)[:, None, :]
    weights = jax.nn.softmax(scores, axis=-1).astype(jnp.bfloat16)
    attended = jnp.einsum(
        "uck,ukd->ucd", weights, centroids, preferred_element_type=jnp.float32
    ).astype(jnp.bfloat16)
    features = jnp.concatenate([candidates, attended], axis=-1).reshape(
        users * local_cands, 2 * width
    )
    hidden = jax.nn.relu(jnp.dot(features, w_hidden, preferred_element_type=jnp.float32) + b_hidden)
    ranking = jnp.dot(hidden, w_out, precision=lax.Precision.HIGHEST)
    return ranking.reshape(users, local_cands)


def on_device(
    behaviors, cluster_ids, lengths, candidates, w_query, w_key, w_hidden, b_hidden, w_out
):
    partials, counts = jax.vmap(cluster_partials)(behaviors, cluster_ids, lengths[:, 0])
    sums, tallies = (
        lax.psum(partials.astype(jnp.bfloat16), "seq").astype(jnp.float32),
        lax.psum(counts.astype(jnp.bfloat16), "seq").astype(jnp.float32),
    )
    centroids, size_bias = statistics(sums, tallies)
    key_rows = make_keys(centroids, w_key)
    mine = lax.all_to_all(candidates, "cand", split_axis=0, concat_axis=1, tiled=True)
    scored = rank_rows(mine, key_rows, centroids, size_bias, w_query, w_hidden, b_hidden, w_out)
    return lax.all_to_all(scored, "cand", split_axis=1, concat_axis=0, tiled=True)


def solution(mesh):
    in_specs = (
        P("cand", "seq", None),
        P("cand", "seq"),
        P("cand", "seq"),
        P(None, ("seq", "cand"), None),
        P(),
        P(),
        P(),
        P(),
        P(),
    )
    out_specs = P(None, ("seq", "cand"))
    return jax.shard_map(
        on_device, mesh=mesh, in_specs=in_specs, out_specs=out_specs, check_vma=False
    )
```

profile of v0, /device:TPU:1, one launch (start us, length us, event | category | flops | bytes accessed | tf_op | source)
XLA Modules:
  0.0 258.1 jit_solution(13973427605766248245)
XLA Ops:
  6.5 6.9 %all-to-all-start = ((bf16[8,32,128]{2,1,0:T(8,128)(2,1)}), bf16[8,32,128]{2,1,0:T(8,128)(2,1)S(1)}, u32[]{:S(2)}, u32[]{:S(2)}) async-start(bf16[8,32,128]{2,1,0:T(8,128)(2,1)} %param.14), calls=%async_computation | async-start | bytes 131072 | tf_op jit(solution)/shard_map/all_to_all | solution.py:82
  13.5 135.2 %while.16 = (s32[]{:T(128)}, f32[1,2048,128]{2,1,0:T(8,128)S(1)}, f32[1,2048]{1,0:T(1,128)S(1)}, s32[16]{0:T(128)S(1)}, s32[1,8192]{1,0:T(1,128)}, /*index=5*/s3...) while((s32[]{:T(128)}, f32[1,2048,128]{2,1,0:T(8,128)S(1)}, ...), condition=%wide.region_2.3_spmd.clone.clone, body=%wide.region_0.2_spmd.clone.clone.sunk | while | flops 547294208 | bytes 5026022 | solution.py:30
  17.0 1.0 dynamic-slice_convert_fusion.2
  18.0 1.5 fusion.66
  19.5 2.5 fusion.67
  25.4 1.0 dynamic-slice_convert_fusion.2
  26.4 1.5 fusion.66
  27.9 2.5 fusion.67
  34.9 1.5 fusion.66
  36.4 2.5 fusion.67
  43.3 1.5 fusion.66
  44.8 2.5 fusion.67
  50.8 1.0 dynamic-slice_convert_fusion.2
  51.8 1.5 fusion.66
  53.3 2.5 fusion.67
  59.2 1.0 dynamic-slice_convert_fusion.2
  60.3 1.5 fusion.66
  61.7 2.5 fusion.67
  67.7 1.0 dynamic-slice_convert_fusion.2
  68.7 1.5 fusion.66
  70.2 2.5 fusion.67
  76.1 1.0 dynamic-slice_convert_fusion.2
  77.2 1.5 fusion.66
  78.6 2.5 fusion.67
  84.6 1.0 dynamic-slice_convert_fusion.2
  85.6 1.5 fusion.66
  87.1 2.5 fusion.67
  94.1 1.5 fusion.66
  95.5 2.5 fusion.67
  102.5 1.5 fusion.66
  104.0 2.5 fusion.67
  109.9 1.0 dynamic-slice_convert_fusion.2
  111.0 1.5 fusion.66
  112.4 2.5 fusion.67
  118.4 1.0 dynamic-slice_convert_fusion.2
  119.4 1.5 fusion.66
  120.9 2.5 fusion.67
  126.8 1.0 dynamic-slice_convert_fusion.2
  127.9 1.5 fusion.66
  129.4 2.5 fusion.67
  136.3 1.5 fusion.66
  137.8 2.5 fusion.67
  144.8 1.5 fusion.66
  146.3 2.5 fusion.67
  149.7 34.1 %psum.15 = bf16[1,2048]{1,0:T(2,128)(2,1)S(1)} all-reduce(bf16[1,2048]{1,0:T(2,128)(2,1)S(1)} %convert_element_type.78), channel_id=1, replica_groups=mesh['seq'=16,'cand'=8] {'seq'}, use_global_device_ids=true, to_apply=%region_4.5 | all-reduce | flops 2048 | bytes 8192 | tf_op jit(solution)/shard_map/psum | solution.py:78
  184.1 50.4 %all-reduce.2.cloned.1.call-done = bf16[1,2048,128]{2,1,0:T(8,128)(2,1)} async-done(((bf16[1,2048,128]{2,1,0:T(8,128)(2,1)}), bf16[1,2048,128]{2,1,0:T(8,128)(2,1)}) %all-reduce.2.cloned.1.call-update) | async-done | bytes 524304 | tf_op jit(solution)/shard_map/psum | solution.py:77
  234.4 1.9 fusion.44
  239.2 11.5 %all_to_all.28 = f32[1,8,32]{2,0,1:T(1,128)S(1)} all-to-all(f32[1,8,32]{2,0,1:T(1,128)S(1)} %all_to_all.23), channel_id=1, replica_groups=mesh['seq'=16,'cand'=8] {'cand'}, dimensions={1} | all-to-all | bytes 2048 | tf_op jit(solution)/shard_map/all_to_all | solution.py:84
  (131 shorter events, 56.8 us)
Async XLA Ops:
  6.5 231.8 %copy-start = (bf16[256,512]{1,0:T(8,128)(2,1)S(1)}, bf16[256,512]{1,0:T(8,128)(2,1)}, u32[]{:S(2)}) copy-start(bf16[256,512]{1,0:T(8,128)(2,1)} %param.17) | copy-start | bytes 786436
  6.5 177.2 %all-to-all-start = ((bf16[8,32,128]{2,1,0:T(8,128)(2,1)}), bf16[8,32,128]{2,1,0:T(8,128)(2,1)S(1)}, u32[]{:S(2)}, u32[]{:S(2)}) async-start(bf16[8,32,128]{2,1,0:T(8,128)(2,1)} %param.14), calls=%async_computation | async-start | bytes 131072 | tf_op jit(solution)/shard_map/all_to_all | solution.py:82
  13.5 221.0 %all-reduce.2.cloned.1.call-start = ((), (), s32[]{:S(2)}) async-start(), calls=%async_computation.2 | async-start | bytes 1048576 | tf_op jit(solution)/shard_map/psum | solution.py:77
  148.7 35.2 %copy-start.1 = (bf16[128,128]{1,0:T(8,128)(2,1)S(1)}, bf16[128,128]{1,0:T(8,128)(2,1)}, u32[]{:S(2)}) copy-start(bf16[128,128]{1,0:T(8,128)(2,1)} %param.15) | copy-start | bytes 98308
  148.7 85.7 %copy-start.5 = (bf16[128,128]{1,0:T(8,128)(2,1)S(1)}, bf16[128,128]{1,0:T(8,128)(2,1)}, u32[]{:S(2)}) copy-start(bf16[128,128]{1,0:T(8,128)(2,1)} %param.16) | copy-start | bytes 98308
  236.3 1.0 copy-start.4
  237.4 1.0 copy-start.2
  237.4 1.2 copy-start.3
Sparse Core Ops, SparseCore 0:
  149.8 84.6 all-reduce.1
where the time goes:
time: 260 us; the launch traced here: 258 us
  matrix products  66.7 us (26%)
  waiting for transfers between devices  50.4 us (19%)
  blocking collectives  45.5 us (18%)
  local copies, waits for them, and re-layouts  38 us (15%)
  other arithmetic  27.1 us (10%)
  between operations  13.5 us (5%)
  loops' own time  9.9 us (4%)
  starting transfers between devices  6.94 us (3%)
    psum x1, waiting for transfers between devices, on_device(): lax.psum(partials.astype(jnp.bfloat16), 'seq').astype(jnp.float32)  50.4 us
    dot_general x16, matrix products, accumulate(): lax.dot_general(onehot, lower, dims, preferred_element_type=jnp.float32)  39.4 us
    psum x1, blocking collectives, on_device(): lax.psum(counts.astype(jnp.bfloat16), 'seq').astype(jnp.float32)  34.1 us
    dot_general x16, matrix products, accumulate(): lax.dot_general(onehot, upper, dims, preferred_element_type=jnp.float32)  23.6 us
    convert_element_type x16, local copies, waits for them, and re-layouts, accumulate(): upper = lax.optimization_barrier(piece.astype(jnp.bfloat16))  16.4 us
    reduce_sum x16, other arithmetic, accumulate(): tallies = tallies + jnp.sum(onehot, axis=0, dtype=jnp.float32)  13.8 us
    all_to_all x1, blocking collectives, on_device(): lax.all_to_all(scored, 'cand', split_axis=1, concat_axis=0, tiled=True)  11.5 us
    while x16, local copies, waits for them, and re-layouts, accumulate(): idents = lax.dynamic_slice_in_dim(cluster_ids, offset, block_rows, 0)  10.9 us
  transfers between devices with their start and end apart: 2, of which 1 were waited for; matrix products, arithmetic and copies ran while one was open for 49% of the time, Pallas kernels for 0%

commit v1 on v0

--- a/solution.py
+++ b/solution.py
@@ -75,7 +75,7 @@
     partials, counts = jax.vmap(cluster_partials)(behaviors, cluster_ids, lengths[:, 0])
     sums, tallies = (
         lax.psum(partials.astype(jnp.bfloat16), "seq").astype(jnp.float32),
-        lax.psum(counts.astype(jnp.bfloat16), "seq").astype(jnp.float32),
+        jnp.sum(lax.all_gather(counts.astype(jnp.bfloat16), "seq"), axis=0).astype(jnp.float32),
     )
     centroids, size_bias = statistics(sums, tallies)
     key_rows = make_keys(centroids, w_key)

time: 260 us -> 260 us (level)
  blocking collectives: 45.5 us -> 30.8 us
  waiting for transfers between devices: 50.4 us -> 65.1 us
    psum x1 -> x0, blocking collectives: 34.1 us -> none  [on_device(): lax.psum(counts.astype(jnp.bfloat16), 'seq').astype(jnp.float32)]
    all_gather x0 -> x1, blocking collectives: none -> 19.3 us  [on_device(): lax.all_gather(counts.astype(jnp.bfloat16), 'seq')]
    psum x1, waiting for transfers between devices: 50.4 us -> 65.1 us  [on_device(): lax.psum(partials.astype(jnp.bfloat16), 'seq').astype(jnp.float32)]
where the time goes in v1:
time: 260 us; the launch traced here: 258 us
  matrix products  66.2 us (25%)
  waiting for transfers between devices  65.1 us (25%)
  local copies, waits for them, and re-layouts  38 us (15%)
  blocking collectives  30.8 us (12%)
  other arithmetic  27.2 us (10%)
  between operations  13.5 us (5%)
  loops' own time  9.89 us (4%)
  starting transfers between devices  6.94 us (3%)
    psum x1, waiting for transfers between devices, on_device(): lax.psum(partials.astype(jnp.bfloat16), 'seq').astype(jnp.float32)  65.1 us
    dot_general x16, matrix products, accumulate(): lax.dot_general(onehot, lower, dims, preferred_element_type=jnp.float32)  39.2 us
    dot_general x16, matrix products, accumulate(): lax.dot_general(onehot, upper, dims, preferred_element_type=jnp.float32)  23.2 us
    all_gather x1, blocking collectives, on_device(): lax.all_gather(counts.astype(jnp.bfloat16), 'seq')  19.3 us
    convert_element_type x16, local copies, waits for them, and re-layouts, accumulate(): upper = lax.optimization_barrier(piece.astype(jnp.bfloat16))  16.4 us
    reduce_sum x16, other arithmetic, accumulate(): tallies = tallies + jnp.sum(onehot, axis=0, dtype=jnp.float32)  13.8 us
    all_to_all x1, blocking collectives, on_device(): lax.all_to_all(scored, 'cand', split_axis=1, concat_axis=0, tiled=True)  11.5 us
    while x16, local copies, waits for them, and re-layouts, accumulate(): idents = lax.dynamic_slice_in_dim(cluster_ids, offset, block_rows, 0)  10.9 us
  transfers between devices with their start and end apart: 2, of which 1 were waited for; matrix products, arithmetic and copies ran while one was open for 49% of the time, Pallas kernels for 0%

profile of v1, /device:TPU:1, one launch (start us, length us, event | category | flops | bytes accessed | tf_op | source)
XLA Modules:
  0.0 257.6 jit_solution(8703952794539358078)
XLA Ops:
  6.5 6.9 %all-to-all-start = ((bf16[8,32,128]{2,1,0:T(8,128)(2,1)}), bf16[8,32,128]{2,1,0:T(8,128)(2,1)S(1)}, u32[]{:S(2)}, u32[]{:S(2)}) async-start(bf16[8,32,128]{2,1,0:T(8,128)(2,1)} %param.14), calls=%async_computation | async-start | bytes 131072 | tf_op jit(solution)/shard_map/all_to_all | solution.py:82
  13.5 134.7 %while.16 = (s32[]{:T(128)}, f32[1,2048,128]{2,1,0:T(8,128)S(1)}, f32[1,2048]{1,0:T(1,128)S(1)}, s32[16]{0:T(128)S(1)}, s32[1,8192]{1,0:T(1,128)}, /*index=5*/s3...) while((s32[]{:T(128)}, f32[1,2048,128]{2,1,0:T(8,128)S(1)}, ...), condition=%wide.region_2.3_spmd.clone.clone, body=%wide.region_0.2_spmd.clone.clone.sunk | while | flops 547294208 | bytes 5026022 | solution.py:30
  17.0 1.0 dynamic-slice_convert_fusion.2
  18.0 1.5 fusion.68
  19.4 2.4 fusion.69
  25.4 1.0 dynamic-slice_convert_fusion.2
  26.4 1.5 fusion.68
  27.9 2.4 fusion.69
  33.8 1.0 dynamic-slice_convert_fusion.2
  34.8 1.5 fusion.68
  36.3 2.4 fusion.69
  43.2 1.5 fusion.68
  44.7 2.4 fusion.69
  50.6 1.0 dynamic-slice_convert_fusion.2
  51.7 1.5 fusion.68
  53.1 2.4 fusion.69
  59.1 1.0 dynamic-slice_convert_fusion.2
  60.1 1.5 fusion.68
  61.5 2.4 fusion.69
  68.5 1.5 fusion.68
  70.0 2.4 fusion.69
  76.9 1.5 fusion.68
  78.4 2.4 fusion.69
  84.3 1.0 dynamic-slice_convert_fusion.2
  85.3 1.5 fusion.68
  86.8 2.4 fusion.69
  92.7 1.0 dynamic-slice_convert_fusion.2
  93.8 1.5 fusion.68
  95.2 2.4 fusion.69
  102.2 1.5 fusion.68
  103.6 2.4 fusion.69
  110.6 1.5 fusion.68
  112.1 2.4 fusion.69
  118.0 1.0 dynamic-slice_convert_fusion.2
  119.0 1.5 fusion.68
  120.5 2.4 fusion.69
  126.4 1.0 dynamic-slice_convert_fusion.2
  127.4 1.5 fusion.68
  128.9 2.4 fusion.69
  134.8 1.0 dynamic-slice_convert_fusion.2
  135.9 1.5 fusion.68
  137.3 2.4 fusion.69
  144.3 1.5 fusion.68
  145.7 2.4 fusion.69
  149.1 19.3 %all-gather.1 = bf16[16,1,2048]{2,1,0:T(2,128)(2,1)S(1)} all-gather(bf16[1,1,2048]{2,1,0:T(2,128)(2,1)S(1)} %convert_bitcast_fusion), channel_id=2, replica_groups=mesh['seq'=16,'cand'=8] {'seq'}, dimensions={0}, use_global_device_ids=true | all-gather | bytes 69632 | tf_op jit(solution)/shard_map/all_gather | solution.py:78
  168.9 65.1 %all-reduce.2.cloned.1.call-done = bf16[1,2048,128]{2,1,0:T(8,128)(2,1)} async-done(((bf16[1,2048,128]{2,1,0:T(8,128)(2,1)}), bf16[1,2048,128]{2,1,0:T(8,128)(2,1)}) %all-reduce.2.cloned.1.call-update) | async-done | bytes 524304 | tf_op jit(solution)/shard_map/psum | solution.py:77
  233.9 1.9 fusion.46
  238.7 11.5 %all_to_all.28 = f32[1,8,32]{2,0,1:T(1,128)S(1)} all-to-all(f32[1,8,32]{2,0,1:T(1,128)S(1)} %all_to_all.23), channel_id=1, replica_groups=mesh['seq'=16,'cand'=8] {'cand'}, dimensions={1} | all-to-all | bytes 2048 | tf_op jit(solution)/shard_map/all_to_all | solution.py:84
  (132 shorter events, 56.9 us)
Async XLA Ops:
  6.5 231.3 %copy-start = (bf16[256,512]{1,0:T(8,128)(2,1)S(1)}, bf16[256,512]{1,0:T(8,128)(2,1)}, u32[]{:S(2)}) copy-start(bf16[256,512]{1,0:T(8,128)(2,1)} %param.17) | copy-start | bytes 786436
  6.5 162.0 %all-to-all-start = ((bf16[8,32,128]{2,1,0:T(8,128)(2,1)}), bf16[8,32,128]{2,1,0:T(8,128)(2,1)S(1)}, u32[]{:S(2)}, u32[]{:S(2)}) async-start(bf16[8,32,128]{2,1,0:T(8,128)(2,1)} %param.14), calls=%async_computation | async-start | bytes 131072 | tf_op jit(solution)/shard_map/all_to_all | solution.py:82
  13.5 220.4 %all-reduce.2.cloned.1.call-start = ((), (), s32[]{:S(2)}) async-start(), calls=%async_computation.2 | async-start | bytes 1048576 | tf_op jit(solution)/shard_map/psum | solution.py:77
  148.2 20.5 %copy-start.1 = (bf16[128,128]{1,0:T(8,128)(2,1)S(1)}, bf16[128,128]{1,0:T(8,128)(2,1)}, u32[]{:S(2)}) copy-start(bf16[128,128]{1,0:T(8,128)(2,1)} %param.15) | copy-start | bytes 98308
  148.2 85.7 %copy-start.5 = (bf16[128,128]{1,0:T(8,128)(2,1)S(1)}, bf16[128,128]{1,0:T(8,128)(2,1)}, u32[]{:S(2)}) copy-start(bf16[128,128]{1,0:T(8,128)(2,1)} %param.16) | copy-start | bytes 98308
  235.8 1.0 copy-start.4
  236.8 1.0 copy-start.2
  236.9 1.3 copy-start.3
Sparse Core Ops, SparseCore 0:
  149.2 84.6 all-reduce.1

commit v2 on v0

--- a/solution.py
+++ b/solution.py
@@ -74,7 +74,7 @@
 ):
     partials, counts = jax.vmap(cluster_partials)(behaviors, cluster_ids, lengths[:, 0])
     sums, tallies = (
-        lax.psum(partials.astype(jnp.bfloat16), "seq").astype(jnp.float32),
+        jnp.sum(lax.all_gather(partials.astype(jnp.bfloat16), "seq"), axis=0).astype(jnp.float32),
         lax.psum(counts.astype(jnp.bfloat16), "seq").astype(jnp.float32),
     )
     centroids, size_bias = statistics(sums, tallies)

time: 260 us -> 251 us (0.965)
  waiting for transfers between devices: 50.4 us -> 33 us
  other arithmetic: 27.1 us -> 33.7 us
  Pallas kernels: 0 us -> 3.16 us
    psum x1 -> x0, waiting for transfers between devices: 50.4 us -> none  [on_device(): lax.psum(partials.astype(jnp.bfloat16), 'seq').astype(jnp.float32)]
    all_gather x0 -> x1, waiting for transfers between devices: none -> 33 us  [on_device(): lax.all_gather(partials.astype(jnp.bfloat16), 'seq')]
    reduce_sum x1, other arithmetic: 0.43 us -> 4.83 us  [on_device(): jnp.sum(lax.all_gather(partials.astype(jnp.bfloat16), 'seq'), axis=0)]
    unnamed x0 -> x1, Pallas kernels: none -> 3.16 us
  transfers between devices with their start and end apart: 2 -> 2, of which waited for: 1 -> 1; matrix products, arithmetic and copies ran while one was open for 49% -> 0% of each run, Pallas kernels for 0% -> 0%
where the time goes in v2:
time: 251 us; the launch traced here: 249 us
  matrix products  65.9 us (26%)
  blocking collectives  44.1 us (18%)
  local copies, waits for them, and re-layouts  38.1 us (15%)
  other arithmetic  33.7 us (13%)
  waiting for transfers between devices  33 us (13%)
  between operations  13.5 us (5%)
  loops' own time  10.7 us (4%)
  starting transfers between devices  6.82 us (3%)
  Pallas kernels  3.16 us (1%)
    dot_general x16, matrix products, accumulate(): lax.dot_general(onehot, lower, dims, preferred_element_type=jnp.float32)  39.4 us
    psum x1, blocking collectives, on_device(): lax.psum(counts.astype(jnp.bfloat16), 'seq').astype(jnp.float32)  34.4 us
    all_gather x1, waiting for transfers between devices, on_device(): lax.all_gather(partials.astype(jnp.bfloat16), 'seq')  33 us
    dot_general x16, matrix products, accumulate(): lax.dot_general(onehot, upper, dims, preferred_element_type=jnp.float32)  23.6 us
    convert_element_type x16, local copies, waits for them, and re-layouts, accumulate(): upper = lax.optimization_barrier(piece.astype(jnp.bfloat16))  16.5 us
    reduce_sum x16, other arithmetic, accumulate(): tallies = tallies + jnp.sum(onehot, axis=0, dtype=jnp.float32)  13.7 us
    while x16, local copies, waits for them, and re-layouts, accumulate(): idents = lax.dynamic_slice_in_dim(cluster_ids, offset, block_rows, 0)  11 us
    another operation x1, loops' own time, cluster_partials(): lax.scan(accumulate, start, jnp.arange(slots // block_rows, dtype=jnp.int...  10.7 us
  transfers between devices with their start and end apart: 2, of which 1 were waited for; matrix products, arithmetic and copies ran while one was open for 0% of the time, Pallas kernels for 0%

profile of v2, /device:TPU:1, one launch (start us, length us, event | category | flops | bytes accessed | tf_op | source)
XLA Modules:
  0.0 249.0 jit_solution(3098183219909804514)
XLA Ops:
  6.6 136.8 %while.16 = (s32[]{:T(128)}, f32[1,2048,128]{2,1,0:T(8,128)S(1)}, f32[1,2048]{1,0:T(1,128)S(1)}, s32[16]{0:T(128)S(1)}, s32[1,8192]{1,0:T(1,128)}, /*index=5*/s3...) while((s32[]{:T(128)}, f32[1,2048,128]{2,1,0:T(8,128)S(1)}, ...), condition=%wide.region_2.3_spmd.clone.clone, body=%wide.region_0.2_spmd.clone.clone.sunk | while | flops 547294208 | bytes 5026014 | solution.py:30
  7.9 1.0 dynamic-slice_convert_fusion.2
  10.3 1.5 fusion.59
  11.7 2.5 fusion.60
  16.4 1.0 dynamic-slice_convert_fusion.2
  18.8 1.5 fusion.59
  20.3 2.5 fusion.60
  25.0 1.0 dynamic-slice_convert_fusion.2
  27.4 1.5 fusion.59
  28.8 2.5 fusion.60
  33.5 1.0 dynamic-slice_convert_fusion.2
  35.9 1.5 fusion.59
  37.4 2.5 fusion.60
  42.1 1.0 dynamic-slice_convert_fusion.2
  44.5 1.5 fusion.59
  45.9 2.5 fusion.60
  50.6 1.0 dynamic-slice_convert_fusion.2
  53.0 1.5 fusion.59
  54.5 2.5 fusion.60
  59.2 1.0 dynamic-slice_convert_fusion.2
  61.6 1.5 fusion.59
  63.0 2.5 fusion.60
  70.1 1.5 fusion.59
  71.6 2.5 fusion.60
  78.7 1.5 fusion.59
  80.1 2.5 fusion.60
  87.2 1.5 fusion.59
  88.7 2.5 fusion.60
  95.8 1.5 fusion.59
  97.2 2.5 fusion.60
  104.3 1.5 fusion.59
  105.8 2.5 fusion.60
  112.9 1.5 fusion.59
  114.3 2.5 fusion.60
  121.4 1.5 fusion.59
  122.9 2.5 fusion.60
  129.9 1.5 fusion.59
  131.4 2.5 fusion.60
  138.5 1.5 fusion.59
  140.0 2.5 fusion.60
  144.2 6.8 %all-to-all-start = ((bf16[8,32,128]{2,1,0:T(8,128)(2,1)}), bf16[8,32,128]{2,1,0:T(8,128)(2,1)S(1)}, u32[]{:S(2)}, u32[]{:S(2)}) async-start(bf16[8,32,128]{2,1,0:T(8,128)(2,1)} %param.14), calls=%async_computation | async-start | bytes 131072 | tf_op jit(solution)/shard_map/all_to_all | solution.py:82
  151.1 34.4 %psum.7 = bf16[1,2048]{1,0:T(2,128)(2,1)S(1)} all-reduce(bf16[1,2048]{1,0:T(2,128)(2,1)S(1)} %convert_element_type.96), channel_id=1, replica_groups=mesh['seq'=16,'cand'=8] {'seq'}, use_global_device_ids=true, to_apply=%region_4.5 | all-reduce | flops 2048 | bytes 8192 | tf_op jit(solution)/shard_map/psum | solution.py:78
  185.7 33.0 %all-gather.3.cloned.1.call-done = bf16[16,2048,128]{2,1,0:T(8,128)(2,1)} async-done(((bf16[1,2048,128]{2,1,0:T(8,128)(2,1)}), bf16[16,2048,128]{2,1,0:T(8,128)(2,1)}) %all-gather.3.cloned.1.call-update) | async-done | bytes 8388624 | tf_op jit(solution)/shard_map/all_gather | solution.py:77
  218.7 4.8 %reduce.7 = bf16[2048,128]{1,0:T(8,128)(2,1)S(1)} reduce(bf16[16,2048,128]{2,1,0:T(8,128)(2,1)} %all-gather.3.cloned.1.call-done, bf16[]{:T(256)} %constant.23.clone.1), dimensions={0}, to_apply=%region_3.4 | reduce | flops 3932160 | bytes 8912898 | tf_op jit(solution)/shard_map/reduce_sum | solution.py:77
  223.6 1.3 convert_divide_fusion
  224.9 2.1 fusion.31
  227.0 3.2 %online-softmax = f32[256,128]{1,0:T(8,128)} custom-call(f32[256,2048]{1,0:T(8,128)} %fusion.31, f32[2048,128]{1,0:T(8,128)} %convert_divide_fusion), custom_call_target="tpu_custom_call" | custom-call | tf_op online-softmax
  231.9 9.7 %all_to_all.28 = f32[1,8,32]{2,0,1:T(1,128)S(1)} all-to-all(f32[1,8,32]{2,0,1:T(1,128)S(1)} %all_to_all.23), channel_id=1, replica_groups=mesh['seq'=16,'cand'=8] {'cand'}, dimensions={1} | all-to-all | bytes 2048 | tf_op jit(solution)/shard_map/all_to_all | solution.py:84
  (130 shorter events, 59.3 us)
Async XLA Ops:
  6.5 224.5 %copy-start = (bf16[256,512]{1,0:T(8,128)(2,1)S(1)}, bf16[256,512]{1,0:T(8,128)(2,1)}, u32[]{:S(2)}) copy-start(bf16[256,512]{1,0:T(8,128)(2,1)} %param.17) | copy-start | bytes 786436
  6.5 212.2 %all-gather.3.cloned.1.call-start = ((), (), s32[]{:S(2)}) async-start(), calls=%async_computation.2 | async-start | bytes 8912896 | tf_op jit(solution)/shard_map/all_gather | solution.py:77
  6.5 179.0 %copy-start.1 = (bf16[128,128]{1,0:T(8,128)(2,1)S(1)}, bf16[128,128]{1,0:T(8,128)(2,1)}, u32[]{:S(2)}) copy-start(bf16[128,128]{1,0:T(8,128)(2,1)} %param.15) | copy-start | bytes 98308
  144.2 41.3 %all-to-all-start = ((bf16[8,32,128]{2,1,0:T(8,128)(2,1)}), bf16[8,32,128]{2,1,0:T(8,128)(2,1)S(1)}, u32[]{:S(2)}, u32[]{:S(2)}) async-start(bf16[8,32,128]{2,1,0:T(8,128)(2,1)} %param.14), calls=%async_computation | async-start | bytes 131072 | tf_op jit(solution)/shard_map/all_to_all | solution.py:82
  185.7 39.2 %copy-start.4 = (bf16[128,128]{1,0:T(8,128)(2,1)S(1)}, bf16[128,128]{1,0:T(8,128)(2,1)}, u32[]{:S(2)}) copy-start(bf16[128,128]{1,0:T(8,128)(2,1)} %param.16) | copy-start | bytes 98308
  224.9 6.2 %copy-start.2 = (f32[512]{0:T(512)S(1)}, f32[512]{0:T(512)}, u32[]{:S(2)}) copy-start(f32[512]{0:T(512)} %param.18) | copy-start | bytes 6148
  224.9 6.4 %copy-start.3 = (f32[512]{0:T(512)S(1)}, f32[512]{0:T(512)}, u32[]{:S(2)}) copy-start(f32[512]{0:T(512)} %param.19) | copy-start | bytes 6148
Sparse Core Ops, SparseCore 0:
  144.4 74.2 all-gather.2
